TPU v7x, 32 devices: a whole 2x2x4 slice. The times are simulated.
32 devices in a mesh: expert: 4 (over z), dp: 4 (over y, core), replica: 2 (over x).
Axes of the slice: x: 2, y: 2, z: 4, core: 2. Of those that a mesh axis runs over, the one named last changes fastest.
Arguments:
- cotangent: bfloat16 [2, 4, 4, 128, 2048], P('replica', 'expert', 'dp'), may hold values from -0.5 to 0.5
- expert_ids: int32 [2, 4, 4, 128, 2], P('replica', 'expert', 'dp'), may hold values from 0 to 3, all different within a row; in each aligned block of 128 rows (0 to 127, 128 to 255, ..., all dimensions but the last counted through in order) at most 96 rows name the same one
- gate_values: float32 [2, 4, 4, 128, 2], P('replica', 'expert', 'dp'), may hold values from 0.1 to 1
- hidden_saved: bfloat16 [2, 4, 4, 4, 4, 24, 7168], P('replica', 'expert', 'dp'), may hold values from -6 to 6
- output_saved: bfloat16 [2, 4, 4, 4, 4, 24, 2048], P('replica', 'expert', 'dp'), may hold values from -6 to 6
- weights: bfloat16 [2, 4, 7168, 2048], P('replica', 'expert', 'dp'), may hold values from -6 to 6
- moment_one: bfloat16 [2, 4, 7168, 2048], P('replica', 'expert', 'dp'), may hold values from -4 to 4
- moment_two: bfloat16 [2, 4, 7168, 2048], P('replica', 'expert', 'dp'), may hold values from 0.19921875 to 2
- anchor: float32 [4, 1792, 2048], P('expert', 'dp'), may hold values from -6 to 6
- outer_moment: float32 [4, 1792, 2048], P('expert', 'dp'), may hold values from -2 to 2
Outputs:
- new_weights: bfloat16 [2, 4, 7168, 2048], P('replica', 'expert', 'dp')
- gate_grads: float32 [2, 4, 4, 128, 2], P('replica', 'expert', 'dp')
- grad_rms: float32 [2], P('replica')
Inputs may be any that keep to these rules, and one draw needn't show every extreme that they name: `expert_ids`: each token names two different experts; among the 128 tokens of one device no expert is named more than 96 times, a bound that some block reaches.
All inputs are finite; a program needn't handle non-finite values.
Results may differ from a plain program's by a relative error of at most 0.0075.
Values may be sent and summed in bfloat16 or wider, within the bound.
A program may use at most 192 MiB of HBM per device.

v0:
```python
import jax
import jax.numpy as jnp
from jax import lax
from jax.sharding import PartitionSpec as P

beta_one = 0.9
beta_two = 0.95
epsilon = 1e-08
inner_rate = 0.3
weight_decay = 0.1
outer_rate = 0.7
nesterov_coef = 0.9


def shards(
    cotangent,
    expert_ids,
    gate_values,
    hidden_saved,
    output_saved,
    weights,
    moment_one,
    moment_two,
    anchor,
    outer_moment,
):
    n_exp = lax.axis_size("expert")
    n_dp = lax.axis_size("dp")
    n_rep = lax.axis_size("replica")
    tok_rows = cotangent.shape[3]
    model_width = cotangent.shape[4]
    capacity = hidden_saved.shape[5]
    hidden_width = hidden_saved.shape[6]
    slots_dev = n_exp * n_dp * capacity
    shard_rows = hidden_width // n_dp
    chosen = expert_ids.reshape(-1)
    onehot = (chosen[:, None] == jnp.arange(n_exp, dtype=jnp.int32)[None, :]).astype(jnp.int32)
    before = jnp.cumsum(onehot, axis=0) - onehot
    order_rank = jnp.sum(before * onehot, axis=1)
    position = (chosen * n_dp + order_rank % n_dp) * capacity + order_rank // n_dp
    stored = output_saved.reshape(n_exp, n_dp, capacity, model_width)
    returned = lax.all_to_all(
        stored.reshape(n_exp * n_dp, capacity, model_width),
        ("expert", "dp"),
        split_axis=0,
        concat_axis=0,
        tiled=True,
    )
    picked = jnp.take(returned.reshape(slots_dev, model_width), position, axis=0).reshape(
        tok_rows, 2, model_width
    )
    upstream = cotangent.reshape(tok_rows, model_width)
    gate_grads = jnp.einsum("tkd,td->tk", picked, upstream, preferred_element_type=jnp.float32)
    gates = gate_values.reshape(tok_rows, 2)
    sends = (gates[:, :, None] * upstream[:, None, :].astype(jnp.float32)).astype(jnp.bfloat16)
    buffer = (
        jnp.zeros((slots_dev, model_width), jnp.bfloat16)
        .at[position]
        .set(sends.reshape(2 * tok_rows, model_width))
    )
    arrived = lax.all_to_all(
        buffer.reshape(n_exp * n_dp, capacity, model_width),
        ("expert", "dp"),
        split_axis=0,
        concat_axis=0,
        tiled=True,
    )
    arrived = arrived.reshape(slots_dev, model_width)
    hidden = hidden_saved.reshape(slots_dev, hidden_width)
    gradient = lax.psum_scatter(
        lax.dot_general(
            hidden, arrived, (((0,), (0,)), ((), ())), preferred_element_type=jnp.float32
        ).astype(jnp.bfloat16),
        "dp",
        scatter_dimension=0,
        tiled=True,
    ).astype(jnp.float32)
    squares = lax.psum(jnp.sum(gradient * gradient), ("expert", "dp"))
    grad_rms = jnp.sqrt(squares / (n_exp * hidden_width * model_width)).reshape(1)
    weight_old = weights.reshape(shard_rows, model_width).astype(jnp.float32)
    first_new = (
        beta_one * moment_one.reshape(shard_rows, model_width).astype(jnp.float32)
        + (1.0 - beta_one) * gradient
    )
    second_new = (
        beta_two * moment_two.reshape(shard_rows, model_width).astype(jnp.float32)
        + (1.0 - beta_two) * gradient * gradient
    )
    inner_new = weight_old - inner_rate * (
        first_new / (jnp.sqrt(second_new) + epsilon) + weight_decay * weight_old
    )
    inner_new = inner_new.astype(jnp.bfloat16)
    grouped = inner_new.reshape(shard_rows // 4, 4, model_width)
    fragment = grouped[:, 0, :].astype(jnp.float32)
    start_point = anchor.reshape(shard_rows // 4, model_width)
    summed = lax.psum((start_point - fragment).astype(jnp.bfloat16), "replica").astype(jnp.float32)
    average = summed / n_rep
    momentum = nesterov_coef * outer_moment.reshape(shard_rows // 4, model_width) + average
    new_anchor = start_point - outer_rate * (average + nesterov_coef * momentum)
    updated = (
        grouped.at[:, 0, :]
        .set(new_anchor.astype(jnp.bfloat16))
        .reshape(1, 1, shard_rows, model_width)
    )
    return (updated, gate_grads.reshape(1, 1, 1, tok_rows, 2), grad_rms)


def solution(mesh):
    return jax.shard_map(
        shards,
        mesh=mesh,
        in_specs=(
            P("replica", "expert", "dp", None, None),
            P("replica", "expert", "dp", None, None),
            P("replica", "expert", "dp", None, None),
            P("replica", "expert", "dp", None, None, None, None),
            P("replica", "expert", "dp", None, None, None, None),
            P("replica", "expert", "dp", None),
            P("replica", "expert", "dp", None),
            P("replica", "expert", "dp", None),
            P("expert", "dp", None),
            P("expert", "dp", None),
        ),
        out_specs=(
            P("replica", "expert", "dp", None),
            P("replica", "expert", "dp", None, None),
            P("replica"),
        ),
        check_vma=False,
    )
```

profile of v0, /device:TPU:0, one launch (start us, length us, event | category | flops | bytes accessed | tf_op | source)
XLA Modules:
  0.0 495.1 jit_solution(3797463655363721530)
XLA Ops:
  8.3 1.2 reduce-window.6
  11.2 2.5 mul.136
  13.7 2.7 mul.137
  16.7 3.5 scatter_custom_fusion
  20.2 43.5 %all_to_all.10 = bf16[16,24,2048]{2,1,0:T(8,128)(2,1)S(1)} all-to-all(bf16[16,24,2048]{2,1,0:T(8,128)(2,1)} %bitcast.83), channel_id=1, replica_groups=mesh['expert'=4,'dp'=4,'replica'=2] {'expert','dp'}, dimensions={0} | all-to-all | bytes 3145728 | tf_op jit(solution)/shard_map/all_to_all | solution.py:61
  63.7 21.7 %convert_bitcast_fusion = bf16[7168,2048]{0,1:T(8,128)(2,1)} fusion(bf16[384,2048]{1,0:T(8,128)(2,1)S(1)} %bitcast.85, bf16[384,7168]{1,0:T(8,128)(2,1)} %bitcast.92), kind=kOutput, calls=%fused_computation.2 | convolution fusion | flops 11288969216 | bytes 36438016 | tf_op jit(solution)/shard_map/dot_general | solution.py:71
  85.4 5.0 %all-to-all-start.1 = ((bf16[16,24,2048]{2,1,0:T(8,128)(2,1)}), bf16[16,24,2048]{2,1,0:T(8,128)(2,1)S(1)}, u32[]{:S(2)}, u32[]{:S(2)}) async-start(bf16[16,24,2048]{2,1,0:T(8,128)(2,1)} %bitcast.84), calls=%async_computation.2 | async-start | bytes 3145728 | tf_op jit(solution)/shard_map/all_to_all | solution.py:42
  90.7 10.7 %copy.33 = bf16[1,1,1792,2048]{2,3,1,0:T(8,128)(2,1)} copy(bf16[1,1,1792,2048]{3,2,1,0:T(8,128)(2,1)} %param.17) | data formatting | bytes 14680064 | tf_op args[5]
  101.4 11.0 %copy.34 = bf16[1,1,1792,2048]{2,3,1,0:T(8,128)(2,1)} copy(bf16[1,1,1792,2048]{3,2,1,0:T(8,128)(2,1)} %param.18) | data formatting | bytes 14680064 | tf_op args[6]
  112.4 10.8 %copy.41 = bf16[1,1,1792,2048]{2,3,1,0:T(8,128)(2,1)} copy(bf16[1,1,1792,2048]{3,2,1,0:T(8,128)(2,1)} %param.19) | data formatting | bytes 14680064 | tf_op args[7]
  123.2 170.8 %reduce-scatter.2.cloned.1.call-done = bf16[1792,2048]{0,1:T(8,128)(2,1)} async-done(((bf16[7168,2048]{0,1:T(8,128)(2,1)}), bf16[1792,2048]{0,1:T(8,128)(2,1)}) %reduce-scatter.2.cloned.1.call-update) | async-done | bytes 7340048 | tf_op jit(solution)/shard_map/reduce_scatter | solution.py:70
  294.0 18.8 %fusion.8 = (f32[]{:T(128)}, bf16[1792,2048]{0,1:T(8,128)(2,1)}) fusion(bf16[1792,2048]{0,1:T(8,128)(2,1)} %reduce-scatter.2.cloned.1.call-done, bf16[1,1,1792,2048]{2,3,1,0:T(8,128)(2,1)} %copy.41, bf16[1,1,1792,2048]{2,3,1,0:T(8,128)(2,1)} %copy.34, bf16[1,1,1792,2048]{2,3,1,0:T(8,128)(2,1)} %copy.33), kind=kLoop, calls=%fused_computation.17 | loop fusion | flops 73400320 | bytes 36700164 | tf_op jit(solution)/shard_map/reduce_sum | solution.py:78
  312.7 10.2 %copy.42 = bf16[1792,2048]{1,0:T(8,128)(2,1)} copy(bf16[1792,2048]{0,1:T(8,128)(2,1)} %get-tuple-element.16) | data formatting | bytes 14680064 | tf_op jit(solution)/shard_map/convert_element_type | solution.py:92
  322.9 11.6 %reshape.232 = bf16[448,4,2048]{2,1,0:T(4,128)(2,1)} reshape(bf16[1792,2048]{1,0:T(8,128)(2,1)} %copy.42) | data formatting | bytes 14680064 | tf_op jit(solution)/shard_map/reshape | solution.py:93
  334.5 8.0 %slice_convert_fusion = f32[448,1,2048]{2,1,0:T(1,128)} fusion(bf16[448,4,2048]{2,1,0:T(4,128)(2,1)} %reshape.232), kind=kLoop, calls=%fused_computation.18 | loop fusion | flops 917504 | bytes 5505024 | tf_op jit(solution)/shard_map/convert_element_type | solution.py:94
  342.5 5.6 %fusion.9 = bf16[448,2048]{1,0:T(8,128)(2,1)} fusion(f32[448,1,2048]{2,1,0:T(1,128)} %slice_convert_fusion, f32[1,448,2048]{2,1,0:T(8,128)} %param.20), kind=kLoop, calls=%fused_computation.20 | loop fusion | flops 1835008 | bytes 9175040 | tf_op jit(solution)/shard_map/convert_element_type | solution.py:96
  348.4 1.4 gather_fusion
  350.5 3.8 fusion.18
  355.0 32.8 %psum.15 = f32[]{:T(128)} all-reduce(f32[]{:T(128)} %get-tuple-element.15), channel_id=1, replica_groups=mesh['expert'=4,'dp'=4,'replica'=2] {'expert','dp'}, use_global_device_ids=true, to_apply=%region_7.8 | all-reduce | flops 1 | bytes 8 | tf_op jit(solution)/shard_map/psum | solution.py:78
  388.5 17.1 %all-reduce.2.cloned.1.call-done = bf16[448,2048]{1,0:T(8,128)(2,1)} async-done(((bf16[448,2048]{1,0:T(8,128)(2,1)}), bf16[448,2048]{1,0:T(8,128)(2,1)}) %all-reduce.2.cloned.1.call-update) | async-done | bytes 1835024 | tf_op jit(solution)/shard_map/psum | solution.py:96
  405.6 4.8 fusion.15
  410.4 4.7 copy.43
  415.1 61.0 %scatter.13 = bf16[448,4,2048]{2,1,0:T(4,128)(2,1)} dynamic-update-slice(bf16[448,4,2048]{2,1,0:T(4,128)(2,1)} %reshape.232, bf16[448,1,2048]{2,1,0:T(2,128)(2,1)} %copy.43, s32[]{:T(128)} %constant.88.clone.1, s32[]{:T(128)} %constant.88.clone.1, s32[]{:T(128)} %constant.88.clone.1) | dynamic-update-slice | bytes 3670020 | tf_op jit(solution)/shard_map/scatter | solution.py:102
  476.1 11.0 %reshape.235 = bf16[1,1,1792,2048]{3,2,1,0:T(8,128)(2,1)} reshape(bf16[448,4,2048]{2,1,0:T(4,128)(2,1)} %scatter.13) | data formatting | bytes 14680064 | tf_op jit(solution)/shard_map/reshape | solution.py:103
  (31 shorter events, 4.9 us)
Async XLA Ops:
  7.2 9.3 %copy-start.1 = (f32[1,1,1,128,2]{3,4,2,1,0:T(2,128)S(1)}, f32[1,1,1,128,2]{3,4,2,1,0:T(2,128)}, u32[]{:S(2)}) copy-start(f32[1,1,1,128,2]{3,4,2,1,0:T(2,128)} %param.14) | copy-start | bytes 3076
  7.2 286.8 %reduce-scatter.2.cloned.1.call-start = ((), (), s32[]{:S(2)}) async-start(), calls=%async_computation.3 | async-start | bytes 36700160 | tf_op jit(solution)/shard_map/reduce_scatter | solution.py:70
  85.4 263.0 %all-to-all-start.1 = ((bf16[16,24,2048]{2,1,0:T(8,128)(2,1)}), bf16[16,24,2048]{2,1,0:T(8,128)(2,1)S(1)}, u32[]{:S(2)}, u32[]{:S(2)}) async-start(bf16[16,24,2048]{2,1,0:T(8,128)(2,1)} %bitcast.84), calls=%async_computation.2 | async-start | bytes 3145728 | tf_op jit(solution)/shard_map/all_to_all | solution.py:42
  90.5 315.1 %all-reduce.2.cloned.1.call-start = ((), (), s32[]{:S(2)}) async-start(), calls=%async_computation.4 | async-start | bytes 3670016 | tf_op jit(solution)/shard_map/psum | solution.py:96
  348.4 2.1 copy-start
Sparse Core Ops, SparseCore 0:
  85.5 208.3 reduce-scatter.1
  348.3 57.2 all-reduce.1
where the time goes:
time: 501 us; the launch traced here: 495 us
  waiting for transfers between devices  188 us (38%)
  local copies, waits for them, and re-layouts  141 us (28%)
  blocking collectives  76.3 us (15%)
  other arithmetic  43.3 us (9%)
  matrix products  25.4 us (5%)
  between operations  16 us (3%)
  starting transfers between devices  5.3 us (1%)
    reduce_scatter x1, waiting for transfers between devices, shards(): lax.psum_scatter(lax.dot_general(hidden, arrived, (((0,), (0,)), ((), ())...  171 us
    scatter x1, local copies, waits for them, and re-layouts, shards(): updated = grouped.at[:, 0, :].set(new_anchor.astype(jnp.bfloat16)).reshap...  61 us
    all_to_all x1, blocking collectives, shards(): lax.all_to_all(buffer.reshape(n_exp * n_dp, capacity, model_width), ('exp...  43.5 us
    unnamed x9, local copies, waits for them, and re-layouts  33.4 us
    psum x1, blocking collectives, shards(): squares = lax.psum(jnp.sum(gradient * gradient), ('expert', 'dp'))  32.8 us
    dot_general x1, matrix products, shards(): lax.dot_general(hidden, arrived, (((0,), (0,)), ((), ())), preferred_elem...  21.7 us
    reduce_sum x1, other arithmetic, shards(): squares = lax.psum(jnp.sum(gradient * gradient), ('expert', 'dp'))  18.8 us
    psum x1, waiting for transfers between devices, shards(): lax.psum((start_point - fragment).astype(jnp.bfloat16), 'replica')  17.1 us
  transfers between devices with their start and end apart: 3, of which 2 were waited for; matrix products, arithmetic and copies ran while one was open for 19% of the time, Pallas kernels for 0%

commit v1 on v0

v1 whole, which is shorter than its diff:
```python
import functools

import jax
import jax.numpy as jnp
from jax import lax
from jax.experimental import pallas as pl
from jax.experimental.pallas import tpu as pltpu
from jax.sharding import PartitionSpec as P

beta_one = 0.9
beta_two = 0.95
epsilon = 1e-08
inner_rate = 0.3
weight_decay = 0.1
outer_rate = 0.7
nesterov_coef = 0.9

MESH = pl.DeviceIdType.MESH
BF = jnp.bfloat16
F32 = jnp.float32


def kernel(
    dims,
    ids_ref, gates_ref, cot_ref, hid_ref, osv_ref, w_ref, m1_ref, m2_ref, anc_ref, om_ref,
    out_ref, gg_ref, rms_ref,
    hid, hidt, slots, sends, wbuf, m1buf, m2buf, ancbuf, ombuf, osv, cot,
    frag_send, frag_recv, tmp, gg_acc, sq_acc, msg_send, msg_recv,
    load_sem, out_sem, hs_sem, hr_sem, zs_sem, zr_sem, ys_sem, yr_sem, ps_sem, pr_sem,
    xs_sem, xr_sem, ms_sem, mr_sem,
):
    n_exp, n_dp, n_rep, cap, rows, width, full, nj, rblk = dims
    dc = width // nj
    n_src = n_exp * n_dp
    per = n_src * cap
    depth = n_dp * per
    n_y = n_dp // 2
    e = lax.axis_index("expert")
    d = lax.axis_index("dp")
    r = lax.axis_index("replica")
    me = e * n_dp + d
    core = lax.rem(d, 2)
    yy = d // 2
    partner = yy * 2 + 1 - core
    other = lax.rem(r + 1, n_rep)

    def cols(j):
        return pl.ds(j * dc, dc)

    def remote(src, dst, ssem, rsem, to):
        return pltpu.make_async_remote_copy(
            src_ref=src, dst_ref=dst, send_sem=ssem, recv_sem=rsem,
            device_id=to, device_id_type=MESH,
        )

    def mod(x, n):
        return lax.rem(x + 2 * n, n)

    loads = []
    for i, (src, dst) in enumerate([
        (cot_ref, cot), (osv_ref, osv), (w_ref, wbuf), (m1_ref, m1buf),
        (m2_ref, m2buf), (anc_ref, ancbuf), (om_ref, ombuf),
    ]):
        loads.append(pltpu.make_async_copy(src, dst, load_sem.at[i]))
    loads[0].start()

    def hid_cols(to):
        return pl.ds(pl.multiple_of(to * rows, 128), rows)

    hid_own = pltpu.make_async_copy(hid_ref.at[:, :, :, hid_cols(d)], hid.at[d], load_sem.at[7])

    barrier = pltpu.get_barrier_semaphore()
    for k in range(1, n_src):
        to = mod(me + k, n_src)
        pl.semaphore_signal(barrier, inc=1, device_id={"expert": to // n_dp, "dp": lax.rem(to, n_dp)}, device_id_type=MESH)
    pl.semaphore_signal(barrier, inc=1, device_id={"replica": other}, device_id_type=MESH)
    pl.semaphore_wait(barrier, n_src)

    hid_sends = []
    for k in range(2, n_dp + 1):
        to = mod(d + k, n_dp) if k < n_dp else partner
        if k < n_dp:
            q = (k - 2) // 2 + 1
            yto = mod(yy + q, n_y)
            to = yto * 2 + lax.rem(k, 2)
        hid_sends.append(remote(
            hid_ref.at[:, :, :, hid_cols(to)], hid.at[d],
            hs_sem.at[k - 2], hr_sem.at[d], {"dp": to},
        ))
        hid_sends[-1].start()
    hid_own.start()
    for c in loads[1:]:
        c.start()

    ids0, ids1 = ids_ref[0:1, :], ids_ref[1:2, :]
    toks = ids_ref.shape[1]
    erow = lax.broadcasted_iota(jnp.int32, (8 * ((n_exp + 7) // 8), toks), 0)
    counts = ((ids0 == erow).astype(F32) + (ids1 == erow).astype(F32)).astype(BF)
    earlier = (
        lax.broadcasted_iota(jnp.int32, (toks, toks), 0) < lax.broadcasted_iota(jnp.int32, (toks, toks), 1)
    ).astype(F32).astype(BF)
    ranks = jnp.dot(counts, earlier, preferred_element_type=F32)
    shift = n_dp.bit_length() - 1

    def place(ids):
        rank = jnp.sum(jnp.where(ids == erow, ranks, 0.0), axis=0, keepdims=True).astype(jnp.int32)
        return (ids * n_dp + (rank & (n_dp - 1))) * cap + (rank >> shift)

    place0, place1 = place(ids0), place(ids1)
    gate0, gate1 = gates_ref[0:1, :], gates_ref[1:2, :]
    srow = lax.broadcasted_iota(jnp.int32, (per, toks), 0)
    gate_slot = jnp.sum(
        jnp.where(srow == place0, gate0, 0.0) + jnp.where(srow == place1, gate1, 0.0), axis=1, keepdims=True
    )
    onehot = ((srow == place0).astype(F32) + (srow == place1).astype(F32)).astype(BF)
    loads[0].wait()
    z_sends = []
    for j in range(nj):
        rows_j = jnp.dot(onehot, cot[:, j * dc:(j + 1) * dc], preferred_element_type=F32)
        sends[:, :, :, j * dc:(j + 1) * dc] = (gate_slot * rows_j).astype(BF).reshape(n_exp, n_dp, cap, dc)
        for k in range(1, n_exp):
            to = mod(e + k, n_exp)
            z_sends.append(remote(
                sends.at[to, :, :, cols(j)], slots.at[:, e, d, :, cols(j)],
                zs_sem.at[k - 1, j], zr_sem.at[e, j], {"expert": to},
            ))
            z_sends[-1].start()
        slots[:, pl.ds(e, 1), pl.ds(d, 1), :, j * dc:(j + 1) * dc] = (
            sends[pl.ds(e, 1), :, :, j * dc:(j + 1) * dc].reshape(n_dp, 1, 1, cap, dc)
        )

    fwd = []
    for j in range(nj):
        for k in range(1, n_exp):
            a = mod(e + k, n_exp)
            remote(
                sends.at[a, :, :, cols(j)], slots.at[:, a, d, :, cols(j)],
                zs_sem.at[k - 1, j], zr_sem.at[a, j], {"expert": a},
            ).wait_recv()
        mine = slots.at[:, :, d, :, cols(j)]
        for q in range(1, n_y):
            to = mod(yy + q, n_y) * 2 + core
            fwd.append(remote(mine, mine, ys_sem.at[q - 1, j], yr_sem.at[yy, j], {"dp": to}))
            fwd[-1].start()
        fwd.append(remote(mine, mine, ps_sem.at[0, j], pr_sem.at[yy, j], {"dp": partner}))
        fwd[-1].start()

    def turn(h):
        for s in range(0, rows, 128):
            block = hid[pl.ds(h, 1), :, :, :, s:s + 128].reshape(per, 128)
            hidt[s:s + 128, pl.ds(pl.multiple_of(h * per, 128), per)] = block.T

    hid_own.wait()
    turn(d)
    for k in range(n_dp, 1, -1):
        if k < n_dp:
            q = (k - 2) // 2 + 1
            h = mod(yy - q, n_y) * 2 + lax.rem(k, 2)
        else:
            h = partner
        remote(hid.at[h], hid.at[h], hs_sem.at[k - 2], hr_sem.at[h], {"dp": h}).wait_recv()
        turn(h)
    for c in loads[1:]:
        c.wait()

    sq_acc[...] = jnp.zeros_like(sq_acc)
    gg_acc[...] = jnp.zeros_like(gg_acc)
    x_sends, outs = [], []
    fblk = rblk // 4

    def main(j):
        lo, hi = j * dc, (j + 1) * dc
        right = slots[:, :, :, :, lo:hi].reshape(depth, dc)
        prod = (
            slots[pl.ds(d, 1), :, :, :, lo:hi].reshape(per, dc).astype(F32)
            * osv[:, :, :, lo:hi].reshape(per, dc).astype(F32)
        )
        part = prod[:, :128]
        for s in range(128, dc, 128):
            part = part + prod[:, s:s + 128]
        gg_acc[...] += part

        def step(i, _):
            here = pl.ds(pl.multiple_of(i * rblk, rblk), rblk)
            g = jnp.dot(hidt[here, :], right, preferred_element_type=F32)
            sq_acc[...] += jnp.sum((g * g).reshape(rblk // 8, 8, dc), axis=0)
            first = beta_one * m1buf[here, lo:hi].astype(F32) + (1.0 - beta_one) * g
            second = beta_two * m2buf[here, lo:hi].astype(F32) + (1.0 - beta_two) * g * g
            old = wbuf[here, lo:hi].astype(F32)
            new = old - inner_rate * (first / (jnp.sqrt(second) + epsilon) + weight_decay * old)
            wbuf[here, lo:hi] = new.astype(BF)
            for s in range(0, dc, 128):
                tmp[s // 128] = new[:, s:s + 128]
                frag_send[pl.ds(pl.multiple_of(i * fblk, fblk), fblk), lo + s:lo + s + 128] = (
                    tmp[s // 128, pl.ds(0, fblk, stride=4), :].astype(BF)
                )
            return 0

        lax.fori_loop(0, rows // rblk, step, 0)
        x_sends.append(remote(
            frag_send.at[:, cols(j)], frag_recv.at[:, cols(j)], xs_sem.at[j], xr_sem.at[j], {"replica": other}
        ))
        x_sends[-1].start()

    def merge(j):
        lo, hi = j * dc, (j + 1) * dc
        x_sends[j].wait_recv()

        def step(i, _):
            here = pl.ds(pl.multiple_of(i * rblk, rblk), rblk)
            there = pl.ds(pl.multiple_of(i * fblk, fblk), fblk)
            start = ancbuf[there, lo:hi]
            summed = (start - frag_send[there, lo:hi].astype(F32)) + (start - frag_recv[there, lo:hi].astype(F32))
            average = summed / n_rep
            momentum = nesterov_coef * ombuf[there, lo:hi] + average
            point = start - outer_rate * (average + nesterov_coef * momentum)
            for s in range(0, dc, 128):
                tmp[s // 128] = wbuf[here, lo + s:lo + s + 128].astype(F32)
                tmp[s // 128, pl.ds(0, fblk, stride=4), :] = point[:, s:s + 128]
                wbuf[here, lo + s:lo + s + 128] = tmp[s // 128].astype(BF)
            return 0

        lax.fori_loop(0, rows // rblk, step, 0)
        outs.append(pltpu.make_async_copy(wbuf.at[:, cols(j)], out_ref.at[:, cols(j)], out_sem.at[j]))
        outs[-1].start()

    for j in range(nj):
        for q in range(1, n_y):
            yfrom = mod(yy - q, n_y)
            got = slots.at[:, :, yfrom * 2 + core, :, cols(j)]
            remote(got, got, ys_sem.at[q - 1, j], yr_sem.at[yfrom, j], {"dp": partner}).wait_recv()
            fwd.append(remote(got, got, ps_sem.at[q, j], pr_sem.at[yfrom, j], {"dp": partner}))
            fwd[-1].start()
        if j >= 2:
            merge(j - 2)
        for q in range(n_y):
            yfrom = mod(yy - q, n_y)
            got = slots.at[:, :, yfrom * 2 + 1 - core, :, cols(j)]
            remote(got, got, ps_sem.at[q, j], pr_sem.at[yfrom, j], {"dp": partner}).wait_recv()
        main(j)

    total = jnp.sum(gg_acc[...], axis=1, keepdims=True)
    msg_send[:, :cap, :] = jnp.broadcast_to(total, (per, 128)).reshape(n_src, cap, 128)
    square = jnp.sum(jnp.sum(sq_acc[...], axis=1, keepdims=True), axis=0, keepdims=True)
    msg_send[:, cap:, :] = jnp.broadcast_to(square.reshape(1, 1, 1), (n_src, 8, 128))
    m_sends = []
    for k in range(1, n_src):
        to = mod(me + k, n_src)
        m_sends.append(remote(
            msg_send.at[to], msg_recv.at[me], ms_sem.at[k - 1], mr_sem.at[me],
            {"expert": to // n_dp, "dp": lax.rem(to, n_dp)},
        ))
        m_sends[-1].start()
    msg_recv[pl.ds(me, 1)] = msg_send[pl.ds(me, 1)]
    if nj >= 2:
        merge(nj - 2)
    for k in range(1, n_src):
        src = mod(me + k, n_src)
        remote(
            msg_recv.at[src], msg_recv.at[src], ms_sem.at[k - 1], mr_sem.at[src],
            {"expert": src // n_dp, "dp": lax.rem(src, n_dp)},
        ).wait_recv()
    dots = msg_recv[:, :cap, :].reshape(per, 128)
    gg_ref[0:1, :] = jnp.sum(jnp.where(srow == place0, dots, 0.0), axis=0, keepdims=True) / gate0
    gg_ref[1:2, :] = jnp.sum(jnp.where(srow == place1, dots, 0.0), axis=0, keepdims=True) / gate1
    squares = jnp.sum(msg_recv[:, cap:, :], axis=0)
    rms_ref[...] = jnp.sqrt(squares / (n_exp * full * width))
    merge(nj - 1)

    for c in hid_sends + z_sends + fwd + x_sends + m_sends:
        c.wait_send()
    for c in outs:
        c.wait()


def shards(
    cotangent, expert_ids, gate_values, hidden_saved, output_saved,
    weights, moment_one, moment_two, anchor, outer_moment,
):
    n_exp = lax.axis_size("expert")
    n_dp = lax.axis_size("dp")
    n_rep = lax.axis_size("replica")
    toks, width = cotangent.shape[3:]
    full = hidden_saved.shape[6]
    rows = full // n_dp
    ids = expert_ids.reshape(toks, 2).T
    gates = gate_values.reshape(toks, 2).T
    hidden = hidden_saved.reshape(hidden_saved.shape[3:])
    stored = output_saved.reshape(output_saved.shape[3:])
    cap = -(-hidden.shape[2] // 8) * 8
    if cap != hidden.shape[2]:
        more = ((0, 0), (0, 0), (0, cap - hidden.shape[2]), (0, 0))
        hidden, stored = jnp.pad(hidden, more), jnp.pad(stored, more)
    nj = 4
    dc = width // nj
    rblk = 256 if rows % 256 == 0 else 128
    n_src = n_exp * n_dp
    n_y = n_dp // 2
    dims = (n_exp, n_dp, n_rep, cap, rows, width, full, nj, rblk)
    anyspace = pl.BlockSpec(memory_space=pl.ANY)
    vmem = pl.BlockSpec(memory_space=pltpu.VMEM)
    dma = pltpu.SemaphoreType.DMA
    per = n_src * cap
    updated, gg, rms = pl.pallas_call(
        functools.partial(kernel, dims),
        out_shape=(
            jax.ShapeDtypeStruct((rows, width), BF),
            jax.ShapeDtypeStruct((2, toks), F32),
            jax.ShapeDtypeStruct((8, 128), F32),
        ),
        in_specs=[vmem, vmem] + [anyspace] * 8,
        out_specs=(anyspace, vmem, vmem),
        scratch_shapes=[
            pltpu.VMEM((n_dp, n_exp, n_dp, cap, rows), BF),
            pltpu.VMEM((rows, n_dp * per), BF),
            pltpu.VMEM((n_dp, n_exp, n_dp, cap, width), BF),
            pltpu.VMEM((n_exp, n_dp, cap, width), BF),
            pltpu.VMEM((rows, width), BF),
            pltpu.VMEM((rows, width), BF),
            pltpu.VMEM((rows, width), BF),
            pltpu.VMEM((rows // 4, width), F32),
            pltpu.VMEM((rows // 4, width), F32),
            pltpu.VMEM((n_exp, n_dp, cap, width), BF),
            pltpu.VMEM((toks, width), BF),
            pltpu.VMEM((rows // 4, width), BF),
            pltpu.VMEM((rows // 4, width), BF),
            pltpu.VMEM((dc // 128, rblk, 128), F32),
            pltpu.VMEM((per, 128), F32),
            pltpu.VMEM((8, dc), F32),
            pltpu.VMEM((n_src, cap + 8, 128), F32),
            pltpu.VMEM((n_src, cap + 8, 128), F32),
            dma((8,)), dma((nj,)), dma((n_dp,)), dma((n_dp,)),
            dma((n_exp, nj)), dma((n_exp, nj)), dma((n_y, nj)), dma((n_y, nj)),
            dma((n_y, nj)), dma((n_y, nj)), dma((nj,)), dma((nj,)),
            dma((n_src,)), dma((n_src,)),
        ],
        compiler_params=pltpu.CompilerParams(
            collective_id=0, has_side_effects=True, vmem_limit_bytes=62 * 1024 * 1024
        ),
        name="step",
    )(
        ids, gates, cotangent.reshape(toks, width), hidden, stored,
        weights.reshape(rows, width), moment_one.reshape(rows, width), moment_two.reshape(rows, width),
        anchor.reshape(rows // 4, width), outer_moment.reshape(rows // 4, width),
    )
    return (
        updated.reshape(1, 1, rows, width),
        gg.T.reshape(1, 1, 1, toks, 2),
        rms[0, :1],
    )


def solution(mesh):
    return jax.shard_map(
        shards,
        mesh=mesh,
        in_specs=(
            P("replica", "expert", "dp", None, None),
            P("replica", "expert", "dp", None, None),
            P("replica", "expert", "dp", None, None),
            P("replica", "expert", "dp", None, None, None, None),
            P("replica", "expert", "dp", None, None, None, None),
            P("replica", "expert", "dp", None),
            P("replica", "expert", "dp", None),
            P("replica", "expert", "dp", None),
            P("expert", "dp", None),
            P("expert", "dp", None),
        ),
        out_specs=(
            P("replica", "expert", "dp", None),
            P("replica", "expert", "dp", None, None),
            P("replica"),
        ),
        check_vma=False,
    )
```

time: 501 us -> 141 us (0.28); the launches traced: 495 us -> 141 us
  waiting for transfers between devices: 188 us -> 0 us
  local copies, waits for them, and re-layouts: 141 us -> 9.28 us
  Pallas kernels: 0 us -> 131 us
  blocking collectives: 76.3 us -> 0 us
  other arithmetic: 43.3 us -> 0 us
  matrix products: 25.4 us -> 0 us
  between operations: 16 us -> 0.64 us
  starting transfers between devices: 5.3 us -> 0 us
    reduce_scatter x1 -> x0, waiting for transfers between devices: 171 us -> none  [shards(): lax.psum_scatter(lax.dot_general(hidden, arrived, (((0,), (0,)), ((), ())...]
    pallas_call x0 -> x1, Pallas kernels: none -> 131 us  [shards(): pl.pallas_call(functools.partial(kernel, dims), out_shape=(jax.ShapeDtype...]
    scatter x1 -> x0, local copies, waits for them, and re-layouts: 61 us -> none  [shards(): updated = grouped.at[:, 0, :].set(new_anchor.astype(jnp.bfloat16)).reshap...]
    all_to_all x1 -> x0, blocking collectives: 43.5 us -> none  [shards(): lax.all_to_all(buffer.reshape(n_exp * n_dp, capacity, model_width), ('exp...]
    psum x1 -> x0, blocking collectives: 32.8 us -> none  [shards(): squares = lax.psum(jnp.sum(gradient * gradient), ('expert', 'dp'))]
    dot_general x2 -> x0, matrix products: 25.4 us -> none  [the longest x1 21.7 us: shards(): lax.dot_general(hidden, arrived, (((0,), (0,)), ((), ())), preferred_elem...]
    unnamed x9 -> x4, local copies, waits for them, and re-layouts: 33.4 us -> 8.09 us
    reshape x2 -> x0, local copies, waits for them, and re-layouts: 22.7 us -> none  [the longest x1 11.6 us: shards(): grouped = inner_new.reshape(shard_rows // 4, 4, model_width)]
  transfers between devices with their start and end apart: 3 -> 0, of which waited for: 2 -> 0; matrix products, arithmetic and copies ran while one was open for 19% -> 0% of each run, Pallas kernels for 0% -> 0%
where the time goes in v1:
time: 141 us
  Pallas kernels  131 us (93%)
  local copies, waits for them, and re-layouts  9.28 us (7%)
    pallas_call x1, Pallas kernels, shards(): pl.pallas_call(functools.partial(kernel, dims), out_shape=(jax.ShapeDtype...  131 us
    unnamed x4, local copies, waits for them, and re-layouts  8.09 us

profile of v1, /device:TPU:0, one launch (start us, length us, event | category | flops | bytes accessed | tf_op | source)
XLA Modules:
  0.0 140.6 jit_solution(17699250458673510048)
XLA Ops:
  0.6 130.7 %step.1 = (bf16[1792,2048]{1,0:T(8,128)(2,1)}, f32[2,128]{1,0:T(2,128)}, f32[8,128]{1,0:T(8,128)}) custom-call(s32[2,128]{1,0:T(2,128)} %bitcast.28, f32[2,128]{1,0:T(2,128)} %bitcast.29, bf16[128,2048]{1,0:T(8,128)(2,1)} %bitcast.27, bf16[4,4,24,7168]{3,2,1,0:T(8,128)(2,1)} %bitcast.23, bf16[4,4,24,2048]{3,2,1,0:T(8,128)(2,1)} %bitcast.26, ...), custom_call_target="tpu_custom_call" | custom-call | tf_op jit(solution)/shard_map/step/pallas_call | solution.py:304
  131.4 1.2 slice.3
  132.5 0.0 copy-start
  132.5 7.5 %copy.15 = bf16[1,1,1792,2048]{3,2,1,0:T(8,128)(2,1)} copy(bf16[1,1,1792,2048]{3,2,1,0:T(8,128)(2,1)} %bitcast.22) | data formatting | bytes 14680064
  140.1 0.0 copy-done
  140.1 0.6 copy.16
Async XLA Ops:
  132.5 7.5 %copy-start = (f32[2,128]{1,0:T(2,128)S(1)}, f32[2,128]{1,0:T(2,128)}, u32[]{:S(2)}) copy-start(f32[2,128]{1,0:T(2,128)} %get-tuple-element.7) | copy-start | bytes 3076

commit v2 on v1

--- a/solution.py
+++ b/solution.py
@@ -25,7 +25,7 @@
     ids_ref, gates_ref, cot_ref, hid_ref, osv_ref, w_ref, m1_ref, m2_ref, anc_ref, om_ref,
     out_ref, gg_ref, rms_ref,
     hid, hidt, slots, sends, wbuf, m1buf, m2buf, ancbuf, ombuf, osv, cot,
-    frag_send, frag_recv, tmp, gg_acc, sq_acc, msg_send, msg_recv,
+    ids_all, gates_all, frag_send, frag_recv, tmp, gg_acc, sq_acc, msg_send, msg_recv,
     load_sem, out_sem, hs_sem, hr_sem, zs_sem, zr_sem, ys_sem, yr_sem, ps_sem, pr_sem,
     xs_sem, xr_sem, ms_sem, mr_sem,
 ):
@@ -58,16 +58,29 @@
 
     loads = []
     for i, (src, dst) in enumerate([
-        (cot_ref, cot), (osv_ref, osv), (w_ref, wbuf), (m1_ref, m1buf),
+        (cot_ref, cot.at[0]), (osv_ref, osv), (w_ref, wbuf), (m1_ref, m1buf),
         (m2_ref, m2buf), (anc_ref, ancbuf), (om_ref, ombuf),
     ]):
         loads.append(pltpu.make_async_copy(src, dst, load_sem.at[i]))
     loads[0].start()
 
-    def hid_cols(to):
-        return pl.ds(pl.multiple_of(to * rows, 128), rows)
-
-    hid_own = pltpu.make_async_copy(hid_ref.at[:, :, :, hid_cols(d)], hid.at[d], load_sem.at[7])
+    split = (rows // rblk + 1) // 2 * rblk
+    halves = ((0, split), (split, rows - split))
+
+    def hid_cols(to, half):
+        start, size = halves[half]
+        return pl.ds(pl.multiple_of(to * rows + start, 128), size)
+
+    def own_rows(half):
+        start, size = halves[half]
+        return pl.ds(start, size)
+
+    hid_own = [
+        pltpu.make_async_copy(
+            hid_ref.at[:, :, :, hid_cols(d, half)], hid.at[d, :, :, :, own_rows(half)], load_sem.at[7 + half]
+        )
+        for half in range(2)
+    ]
 
     barrier = pltpu.get_barrier_semaphore()
     for k in range(1, n_src):
@@ -76,109 +89,145 @@
     pl.semaphore_signal(barrier, inc=1, device_id={"replica": other}, device_id_type=MESH)
     pl.semaphore_wait(barrier, n_src)
 
+    y_sends = []
+    for q in range(1, n_y):
+        to = mod(yy + q, n_y) * 2 + core
+        for i, (src, dst) in enumerate([(ids_ref, ids_all), (gates_ref, gates_all), (cot_ref, cot)]):
+            y_sends.append(remote(src, dst.at[q], ys_sem.at[i, q], yr_sem.at[i, q], {"dp": to}))
+            y_sends[-1].start()
+
+    def peer(k, sign):
+        if k == n_dp:
+            return partner
+        return mod(yy + sign * ((k - 2) // 2 + 1), n_y) * 2 + lax.rem(k, 2)
+
     hid_sends = []
-    for k in range(2, n_dp + 1):
-        to = mod(d + k, n_dp) if k < n_dp else partner
-        if k < n_dp:
-            q = (k - 2) // 2 + 1
-            yto = mod(yy + q, n_y)
-            to = yto * 2 + lax.rem(k, 2)
-        hid_sends.append(remote(
-            hid_ref.at[:, :, :, hid_cols(to)], hid.at[d],
-            hs_sem.at[k - 2], hr_sem.at[d], {"dp": to},
-        ))
-        hid_sends[-1].start()
-    hid_own.start()
+    for half in range(2):
+        for k in range(2, n_dp + 1):
+            to = peer(k, 1)
+            hid_sends.append(remote(
+                hid_ref.at[:, :, :, hid_cols(to, half)], hid.at[d, :, :, :, own_rows(half)],
+                hs_sem.at[half, k - 2], hr_sem.at[half, d], {"dp": to},
+            ))
+            hid_sends[-1].start()
+        hid_own[half].start()
     for c in loads[1:]:
         c.start()
 
-    ids0, ids1 = ids_ref[0:1, :], ids_ref[1:2, :]
     toks = ids_ref.shape[1]
     erow = lax.broadcasted_iota(jnp.int32, (8 * ((n_exp + 7) // 8), toks), 0)
-    counts = ((ids0 == erow).astype(F32) + (ids1 == erow).astype(F32)).astype(BF)
     earlier = (
         lax.broadcasted_iota(jnp.int32, (toks, toks), 0) < lax.broadcasted_iota(jnp.int32, (toks, toks), 1)
     ).astype(F32).astype(BF)
-    ranks = jnp.dot(counts, earlier, preferred_element_type=F32)
+    srow = lax.broadcasted_iota(jnp.int32, (per, toks), 0)
     shift = n_dp.bit_length() - 1
 
-    def place(ids):
-        rank = jnp.sum(jnp.where(ids == erow, ranks, 0.0), axis=0, keepdims=True).astype(jnp.int32)
-        return (ids * n_dp + (rank & (n_dp - 1))) * cap + (rank >> shift)
-
-    place0, place1 = place(ids0), place(ids1)
-    gate0, gate1 = gates_ref[0:1, :], gates_ref[1:2, :]
-    srow = lax.broadcasted_iota(jnp.int32, (per, toks), 0)
-    gate_slot = jnp.sum(
-        jnp.where(srow == place0, gate0, 0.0) + jnp.where(srow == place1, gate1, 0.0), axis=1, keepdims=True
-    )
-    onehot = ((srow == place0).astype(F32) + (srow == place1).astype(F32)).astype(BF)
-    loads[0].wait()
+    def places(both):
+        counts = ((both[0:1] == erow).astype(F32) + (both[1:2] == erow).astype(F32)).astype(BF)
+        ranks = jnp.dot(counts, earlier, preferred_element_type=F32)
+
+        def place(ids):
+            rank = jnp.sum(jnp.where(ids == erow, ranks, 0.0), axis=0, keepdims=True).astype(jnp.int32)
+            return (ids * n_dp + (rank & (n_dp - 1))) * cap + (rank >> shift)
+
+        return place(both[0:1]), place(both[1:2])
+
+    def table(both, gates):
+        place0, place1 = places(both)
+        gate_slot = jnp.sum(
+            jnp.where(srow == place0, gates[0:1], 0.0) + jnp.where(srow == place1, gates[1:2], 0.0),
+            axis=1, keepdims=True,
+        )
+        return ((srow == place0).astype(F32) + (srow == place1).astype(F32)).astype(BF), gate_slot
+
     z_sends = []
-    for j in range(nj):
-        rows_j = jnp.dot(onehot, cot[:, j * dc:(j + 1) * dc], preferred_element_type=F32)
-        sends[:, :, :, j * dc:(j + 1) * dc] = (gate_slot * rows_j).astype(BF).reshape(n_exp, n_dp, cap, dc)
+
+    def fill(q, j, onehot, gate_slot):
+        lo, hi = j * dc, (j + 1) * dc
+        row = mod(yy - q, n_y)
+        rows_j = jnp.dot(onehot, cot[q, :, lo:hi], preferred_element_type=F32)
+        sends[q, :, :, :, lo:hi] = (gate_slot * rows_j).astype(BF).reshape(n_exp, n_dp, cap, dc)
         for k in range(1, n_exp):
             to = mod(e + k, n_exp)
             z_sends.append(remote(
-                sends.at[to, :, :, cols(j)], slots.at[:, e, d, :, cols(j)],
-                zs_sem.at[k - 1, j], zr_sem.at[e, j], {"expert": to},
+                sends.at[q, to, :, :, cols(j)], slots.at[:, e, row, core, :, cols(j)],
+                zs_sem.at[q, k - 1, j], zr_sem.at[q, e, j], {"expert": to},
             ))
             z_sends[-1].start()
-        slots[:, pl.ds(e, 1), pl.ds(d, 1), :, j * dc:(j + 1) * dc] = (
-            sends[pl.ds(e, 1), :, :, j * dc:(j + 1) * dc].reshape(n_dp, 1, 1, cap, dc)
-        )
+        slots[:, pl.ds(e, 1), pl.ds(row, 1), pl.ds(core, 1), :, lo:hi] = (
+            sends[q, pl.ds(e, 1), :, :, lo:hi].reshape(n_dp, 1, 1, 1, cap, dc)
+        )
+
+    loads[0].wait()
+    tables = [table(ids_ref[...], gates_ref[...])]
+    fill(0, 0, *tables[0])
+    if nj > 1:
+        fill(0, 1, *tables[0])
+    for q in range(1, n_y):
+        h = mod(yy - q, n_y) * 2 + core
+        for i, (src, dst) in enumerate([(ids_ref, ids_all), (gates_ref, gates_all), (cot_ref, cot)]):
+            remote(src, dst.at[q], ys_sem.at[i, q], yr_sem.at[i, q], {"dp": h}).wait_recv()
+        tables.append(table(ids_all[q], gates_all[q]))
+    for j in range(nj):
+        for q in range(n_y):
+            if q > 0 or j > 1:
+                fill(q, j, *tables[q])
 
     fwd = []
-    for j in range(nj):
+
+    def column(j):
         for k in range(1, n_exp):
             a = mod(e + k, n_exp)
-            remote(
-                sends.at[a, :, :, cols(j)], slots.at[:, a, d, :, cols(j)],
-                zs_sem.at[k - 1, j], zr_sem.at[a, j], {"expert": a},
-            ).wait_recv()
-        mine = slots.at[:, :, d, :, cols(j)]
-        for q in range(1, n_y):
-            to = mod(yy + q, n_y) * 2 + core
-            fwd.append(remote(mine, mine, ys_sem.at[q - 1, j], yr_sem.at[yy, j], {"dp": to}))
-            fwd[-1].start()
-        fwd.append(remote(mine, mine, ps_sem.at[0, j], pr_sem.at[yy, j], {"dp": partner}))
+            for q in range(n_y):
+                remote(
+                    sends.at[q, a, :, :, cols(j)], slots.at[:, a, mod(yy - q, n_y), core, :, cols(j)],
+                    zs_sem.at[q, k - 1, j], zr_sem.at[q, a, j], {"expert": a},
+                ).wait_recv()
+        mine = slots.at[:, :, :, core, :, cols(j)]
+        fwd.append(remote(mine, mine, ps_sem.at[j], pr_sem.at[j], {"dp": partner}))
         fwd[-1].start()
 
-    def turn(h):
-        for s in range(0, rows, 128):
+    def partner_column(j):
+        got = slots.at[:, :, :, 1 - core, :, cols(j)]
+        remote(got, got, ps_sem.at[j], pr_sem.at[j], {"dp": partner}).wait_recv()
+
+    def turn(h, half):
+        start, size = halves[half]
+        for s in range(start, start + size, 128):
             block = hid[pl.ds(h, 1), :, :, :, s:s + 128].reshape(per, 128)
             hidt[s:s + 128, pl.ds(pl.multiple_of(h * per, 128), per)] = block.T
 
-    hid_own.wait()
-    turn(d)
-    for k in range(n_dp, 1, -1):
-        if k < n_dp:
-            q = (k - 2) // 2 + 1
-            h = mod(yy - q, n_y) * 2 + lax.rem(k, 2)
-        else:
-            h = partner
-        remote(hid.at[h], hid.at[h], hs_sem.at[k - 2], hr_sem.at[h], {"dp": h}).wait_recv()
-        turn(h)
-    for c in loads[1:]:
-        c.wait()
+    def near(half):
+        hid_own[half].wait()
+        turn(d, half)
+
+    def far(half):
+        for k in range(n_dp, 1, -1):
+            h = peer(k, -1)
+            dst = hid.at[h, :, :, :, own_rows(half)]
+            remote(dst, dst, hs_sem.at[half, k - 2], hr_sem.at[half, h], {"dp": h}).wait_recv()
+            turn(h, half)
 
     sq_acc[...] = jnp.zeros_like(sq_acc)
     gg_acc[...] = jnp.zeros_like(gg_acc)
-    x_sends, outs = [], []
+    x_sends, outs = {}, []
     fblk = rblk // 4
 
-    def main(j):
+    def products(j):
         lo, hi = j * dc, (j + 1) * dc
-        right = slots[:, :, :, :, lo:hi].reshape(depth, dc)
         prod = (
-            slots[pl.ds(d, 1), :, :, :, lo:hi].reshape(per, dc).astype(F32)
+            slots[pl.ds(d, 1), :, :, :, :, lo:hi].reshape(per, dc).astype(F32)
             * osv[:, :, :, lo:hi].reshape(per, dc).astype(F32)
         )
         part = prod[:, :128]
         for s in range(128, dc, 128):
             part = part + prod[:, s:s + 128]
         gg_acc[...] += part
+
+    def main(half, j):
+        lo, hi = j * dc, (j + 1) * dc
+        start, size = halves[half]
+        right = slots[:, :, :, :, :, lo:hi].reshape(depth, dc)
 
         def step(i, _):
             here = pl.ds(pl.multiple_of(i * rblk, rblk), rblk)
@@ -196,15 +245,22 @@
                 )
             return 0
 
-        lax.fori_loop(0, rows // rblk, step, 0)
-        x_sends.append(remote(
-            frag_send.at[:, cols(j)], frag_recv.at[:, cols(j)], xs_sem.at[j], xr_sem.at[j], {"replica": other}
-        ))
-        x_sends[-1].start()
-
-    def merge(j):
+        lax.fori_loop(start // rblk, (start + size) // rblk, step, 0)
+        part = frag_part(half)
+        x_sends[half, j] = remote(
+            frag_send.at[part, cols(j)], frag_recv.at[part, cols(j)],
+            xs_sem.at[half, j], xr_sem.at[half, j], {"replica": other},
+        )
+        x_sends[half, j].start()
+
+    def frag_part(half):
+        start, size = halves[half]
+        return pl.ds(start // 4, size // 4)
+
+    def merge(half, j):
         lo, hi = j * dc, (j + 1) * dc
-        x_sends[j].wait_recv()
+        start_row, size = halves[half]
+        x_sends[half, j].wait_recv()
 
         def step(i, _):
             here = pl.ds(pl.multiple_of(i * rblk, rblk), rblk)
@@ -220,24 +276,47 @@
                 wbuf[here, lo + s:lo + s + 128] = tmp[s // 128].astype(BF)
             return 0
 
-        lax.fori_loop(0, rows // rblk, step, 0)
-        outs.append(pltpu.make_async_copy(wbuf.at[:, cols(j)], out_ref.at[:, cols(j)], out_sem.at[j]))
+        lax.fori_loop(start_row // rblk, (start_row + size) // rblk, step, 0)
+        whole = own_rows(half)
+        outs.append(pltpu.make_async_copy(
+            wbuf.at[whole, cols(j)], out_ref.at[whole, cols(j)], out_sem.at[half, j]
+        ))
         outs[-1].start()
 
-    for j in range(nj):
-        for q in range(1, n_y):
-            yfrom = mod(yy - q, n_y)
-            got = slots.at[:, :, yfrom * 2 + core, :, cols(j)]
-            remote(got, got, ys_sem.at[q - 1, j], yr_sem.at[yfrom, j], {"dp": partner}).wait_recv()
-            fwd.append(remote(got, got, ps_sem.at[q, j], pr_sem.at[yfrom, j], {"dp": partner}))
-            fwd[-1].start()
-        if j >= 2:
-            merge(j - 2)
-        for q in range(n_y):
-            yfrom = mod(yy - q, n_y)
-            got = slots.at[:, :, yfrom * 2 + 1 - core, :, cols(j)]
-            remote(got, got, ps_sem.at[q, j], pr_sem.at[yfrom, j], {"dp": partner}).wait_recv()
-        main(j)
+    near(0)
+    column(0)
+    far(0)
+    for c in loads[1:]:
+        c.wait()
+    last = nj - 1
+    order = []
+    for j in range(last):
+        if j > 0:
+            column(j)
+        partner_column(j)
+        products(j)
+        main(0, j)
+        order.append((0, j))
+        if j == 0:
+            near(1)
+        if j > 0:
+            merge(*order[j - 1])
+    merged = last - 1
+    far(1)
+    column(last)
+    for j in range(last):
+        main(1, j)
+        order.append((1, j))
+        merge(*order[merged])
+        merged += 1
+    partner_column(last)
+    products(last)
+    for half in range(2):
+        main(half, last)
+        order.append((half, last))
+        if half == 0:
+            merge(*order[merged])
+            merged += 1
 
     total = jnp.sum(gg_acc[...], axis=1, keepdims=True)
     msg_send[:, :cap, :] = jnp.broadcast_to(total, (per, 128)).reshape(n_src, cap, 128)
@@ -252,22 +331,25 @@
         ))
         m_sends[-1].start()
     msg_recv[pl.ds(me, 1)] = msg_send[pl.ds(me, 1)]
-    if nj >= 2:
-        merge(nj - 2)
+    while merged < len(order) - 1:
+        merge(*order[merged])
+        merged += 1
     for k in range(1, n_src):
         src = mod(me + k, n_src)
         remote(
             msg_recv.at[src], msg_recv.at[src], ms_sem.at[k - 1], mr_sem.at[src],
             {"expert": src // n_dp, "dp": lax.rem(src, n_dp)},
         ).wait_recv()
+    place0, place1 = places(ids_ref[...])
+    gate0, gate1 = gates_ref[0:1, :], gates_ref[1:2, :]
     dots = msg_recv[:, :cap, :].reshape(per, 128)
     gg_ref[0:1, :] = jnp.sum(jnp.where(srow == place0, dots, 0.0), axis=0, keepdims=True) / gate0
     gg_ref[1:2, :] = jnp.sum(jnp.where(srow == place1, dots, 0.0), axis=0, keepdims=True) / gate1
     squares = jnp.sum(msg_recv[:, cap:, :], axis=0)
     rms_ref[...] = jnp.sqrt(squares / (n_exp * full * width))
-    merge(nj - 1)
-
-    for c in hid_sends + z_sends + fwd + x_sends + m_sends:
+    merge(*order[merged])
+
+    for c in y_sends + hid_sends + z_sends + fwd + list(x_sends.values()) + m_sends:
         c.wait_send()
     for c in outs:
         c.wait()
@@ -313,15 +395,17 @@
         scratch_shapes=[
             pltpu.VMEM((n_dp, n_exp, n_dp, cap, rows), BF),
             pltpu.VMEM((rows, n_dp * per), BF),
-            pltpu.VMEM((n_dp, n_exp, n_dp, cap, width), BF),
-            pltpu.VMEM((n_exp, n_dp, cap, width), BF),
+            pltpu.VMEM((n_dp, n_exp, n_y, 2, cap, width), BF),
+            pltpu.VMEM((n_y, n_exp, n_dp, cap, width), BF),
             pltpu.VMEM((rows, width), BF),
             pltpu.VMEM((rows, width), BF),
             pltpu.VMEM((rows, width), BF),
             pltpu.VMEM((rows // 4, width), F32),
             pltpu.VMEM((rows // 4, width), F32),
             pltpu.VMEM((n_exp, n_dp, cap, width), BF),
-            pltpu.VMEM((toks, width), BF),
+            pltpu.VMEM((n_y, toks, width), BF),
+            pltpu.VMEM((n_y, 2, toks), jnp.int32),
+            pltpu.VMEM((n_y, 2, toks), F32),
             pltpu.VMEM((rows // 4, width), BF),
             pltpu.VMEM((rows // 4, width), BF),
             pltpu.VMEM((dc // 128, rblk, 128), F32),
@@ -329,9 +413,9 @@
             pltpu.VMEM((8, dc), F32),
             pltpu.VMEM((n_src, cap + 8, 128), F32),
             pltpu.VMEM((n_src, cap + 8, 128), F32),
-            dma((8,)), dma((nj,)), dma((n_dp,)), dma((n_dp,)),
-            dma((n_exp, nj)), dma((n_exp, nj)), dma((n_y, nj)), dma((n_y, nj)),
-            dma((n_y, nj)), dma((n_y, nj)), dma((nj,)), dma((nj,)),
+            dma((9,)), dma((2, nj)), dma((2, n_dp)), dma((2, n_dp)),
+            dma((n_y, n_exp, nj)), dma((n_y, n_exp, nj)), dma((3, n_y)), dma((3, n_y)),
+            dma((nj,)), dma((nj,)), dma((2, nj)), dma((2, nj)),
             dma((n_src,)), dma((n_src,)),
         ],
         compiler_params=pltpu.CompilerParams(

time: 141 us -> 120 us (0.85)
  Pallas kernels: 131 us -> 109 us
    pallas_call x1, Pallas kernels: 131 us -> 109 us  [shards(): pl.pallas_call(functools.partial(kernel, dims), out_shape=(jax.ShapeDtype...]
where the time goes in v2:
time: 120 us; the launch traced here: 119 us
  Pallas kernels  109 us (91%)
  local copies, waits for them, and re-layouts  9.28 us (8%)
    pallas_call x1, Pallas kernels, shards(): pl.pallas_call(functools.partial(kernel, dims), out_shape=(jax.ShapeDtype...  109 us
    unnamed x4, local copies, waits for them, and re-layouts  8.09 us

profile of v2, /device:TPU:0, one launch (start us, length us, event | category | flops | bytes accessed | tf_op | source)
XLA Modules:
  0.0 118.7 jit_solution(14205679917926279612)
XLA Ops:
  0.6 108.8 %step.1 = (bf16[1792,2048]{1,0:T(8,128)(2,1)}, f32[2,128]{1,0:T(2,128)}, f32[8,128]{1,0:T(8,128)}) custom-call(s32[2,128]{1,0:T(2,128)} %bitcast.28, f32[2,128]{1,0:T(2,128)} %bitcast.29, bf16[128,2048]{1,0:T(8,128)(2,1)} %bitcast.27, bf16[4,4,24,7168]{3,2,1,0:T(8,128)(2,1)} %bitcast.23, bf16[4,4,24,2048]{3,2,1,0:T(8,128)(2,1)} %bitcast.26, ...), custom_call_target="tpu_custom_call" | custom-call | tf_op jit(solution)/shard_map/step/pallas_call | solution.py:386
  109.5 1.2 %slice.3 = f32[1,1]{1,0:T(1,128)} slice(f32[8,128]{1,0:T(8,128)} %get-tuple-element.8), slice={[0:1], [0:1]} | slice | bytes 8 | tf_op jit(solution)/shard_map/slice | solution.py:433
  110.7 0.0 copy-start
  110.7 7.5 %copy.15 = bf16[1,1,1792,2048]{3,2,1,0:T(8,128)(2,1)} copy(bf16[1,1,1792,2048]{3,2,1,0:T(8,128)(2,1)} %bitcast.22) | data formatting | bytes 14680064
  118.2 0.0 copy-done
  118.2 0.6 copy.16
Async XLA Ops:
  110.7 7.5 %copy-start = (f32[2,128]{1,0:T(2,128)S(1)}, f32[2,128]{1,0:T(2,128)}, u32[]{:S(2)}) copy-start(f32[2,128]{1,0:T(2,128)} %get-tuple-element.7) | copy-start | bytes 3076
